TPU v7x, 256 devices: a whole 4x4x8 slice. The times are simulated.
256 devices in a mesh: prow: 32 (over z_hi, y, x), pcol: 8 (over z_lo, core).
Axes of the slice: x: 4, y: 4, z: 8 (z_hi: 2, z_lo: 4; z = z_hi * 4 + z_lo), core: 2. Of those that a mesh axis runs over, the one named last changes fastest.
Arguments:
- eigen_rows: float32 [1024, 229376], P(('pcol', 'prow')), may hold values from -6 to 6
- reflectors: float32 [229376, 512], P('prow', 'pcol'), may hold values from -0.375 to 0.375
- tfactors: float32 [2, 256, 256], replicated, may hold values from -0.01171875 to 0.01171875
Outputs:
- back_rows: float32 [1024, 229376], P('pcol', 'prow')
All inputs are finite; a program needn't handle non-finite values.
Results may differ from a plain program's by a relative error of at most 0.000084.
Values sent between devices are 32-bit elements; how exact they have to be, the bound alone decides.
No kernel may reach another device: no remote copies, remote signals or barrier semaphores. Data moves between devices by JAX's collectives and lax.ppermute only.
A program may use at most 128 MiB of HBM per device.

v0:
```python
import jax
import jax.numpy as jnp
from jax import lax
from jax.sharding import PartitionSpec as P


def upper_part(square):
    width = square.shape[0]
    rows = lax.broadcasted_iota(jnp.int32, (width, width), 0)
    cols = lax.broadcasted_iota(jnp.int32, (width, width), 1)
    return jnp.where(cols >= rows, square, jnp.zeros_like(square))


def matmul(left, right, precision=lax.Precision.HIGHEST):
    return jnp.dot(left, right, precision=precision, preferred_element_type=jnp.float32)


def sum_over_prow(values, members):
    slices = values.reshape((members, -1, 128))
    received = lax.all_to_all(slices, "prow", split_axis=0, concat_axis=0, tiled=True)
    total = jnp.sum(received, axis=0, keepdims=True)
    copies = jnp.broadcast_to(total, slices.shape)
    return lax.all_to_all(copies, "prow", split_axis=0, concat_axis=0, tiled=True)


def body(eigen_rows, reflectors, tfactors):
    members = lax.axis_size("prow")
    width = tfactors.shape[1]
    vectors = lax.all_gather(reflectors, "pcol", axis=1, tiled=True)
    rows = lax.all_to_all(eigen_rows, "prow", split_axis=1, concat_axis=0, tiled=True)
    count = rows.shape[0]
    first_tri = upper_part(tfactors[0])
    second_tri = upper_part(tfactors[1])
    fast = lax.Precision.HIGH
    projected = matmul(rows, vectors, fast)
    cross = matmul(vectors[:, width:].T, vectors[:, :width], fast)
    packed = jnp.concatenate([projected.reshape(members, -1), cross.reshape(members, -1)], axis=1)
    packed = sum_over_prow(packed, members).reshape(packed.shape)
    split = projected.size // members
    projected = packed[:, :split].reshape(count, 2 * width)
    cross = packed[:, split:].reshape(width, width)
    scaled_second = matmul(projected[:, width:], second_tri.T)
    first = projected[:, :width] - matmul(scaled_second, cross)
    scaled_first = matmul(first, first_tri.T)
    scaled = jnp.concatenate([scaled_first, scaled_second], axis=1)
    return rows - matmul(scaled, vectors.T, fast)


def solution(mesh):
    return jax.shard_map(
        body,
        mesh=mesh,
        in_specs=(P(("pcol", "prow"), None), P("prow", "pcol"), P()),
        out_specs=P("pcol", "prow"),
        check_vma=False,
    )
```

profile of v0, /device:TPU:32, one launch (start us, length us, event | category | flops | bytes accessed | tf_op | source)
XLA Modules:
  0.0 336.6 jit_solution(14484541034405303866)
XLA Ops:
  6.5 0.0 all-gather.2.cloned.1.call-start
  6.5 0.7 all-gather.2.cloned.1.call-update
  7.3 139.8 %all_to_all.29 = f32[4,32,7168]{2,0,1:T(4,128)} all-to-all(f32[4,32,7168]{2,0,1:T(4,128)} %bitcast.19), channel_id=1, replica_groups=mesh['prow'=32,'pcol'=8] {'prow'}, dimensions={1} | all-to-all | bytes 7340032 | tf_op jit(solution)/shard_map/all_to_all | solution.py:30
  147.0 5.3 %all_to_all.23 = f32[128,7168]{1,0:T(8,128)} reshape(f32[32,4,7168]{2,1,0:T(4,128)} %bitcast.18) | data formatting | bytes 7340032 | tf_op jit(solution)/shard_map/all_to_all | solution.py:30
  152.3 86.0 %all-gather.2.cloned.1.call-done = f32[7168,512]{0,1:T(8,128)} async-done(((f32[7168,64]{0,1:T(8,128)}), f32[7168,512]{0,1:T(8,128)}) %all-gather.2.cloned.1.call-update) | async-done | bytes 14680080 | tf_op jit(solution)/shard_map/all_gather | solution.py:29
  238.3 11.7 %fusion = f32[256,256]{1,0:T(8,128)S(1)} fusion(f32[7168,512]{0,1:T(8,128)} %all-gather.2.cloned.1.call-done), kind=kOutput, calls=%fused_computation.1 | convolution fusion | flops 2818572288 | bytes 14942208 | tf_op jit(solution)/shard_map/dot_general | solution.py:15
  250.0 11.8 %fusion.17 = f32[128,512]{1,0:T(8,128)S(1)} fusion(f32[128,7168]{1,0:T(8,128)} %all_to_all.23, f32[7168,512]{0,1:T(8,128)} %all-gather.2.cloned.1.call-done), kind=kOutput, calls=%fused_computation.24 | convolution fusion | flops 2818572288 | bytes 18612224 | tf_op jit(solution)/shard_map/dot_general | solution.py:15
  261.9 0.0 copy-start
  261.9 0.1 pad_maximum_fusion
  262.0 32.9 %all_to_all.30 = f32[32,32,128]{2,1,0:T(8,128)S(1)} all-to-all(f32[32,32,128]{2,1,0:T(8,128)S(1)} %pad_maximum_fusion), channel_id=1, replica_groups=mesh['prow'=32,'pcol'=8] {'prow'}, dimensions={0} | all-to-all | bytes 1048576 | tf_op jit(solution)/shard_map/all_to_all | solution.py:20
  294.9 0.1 broadcast_in_dim.2
  295.0 20.4 %all_to_all.31 = f32[32,32,128]{2,1,0:T(8,128)S(1)} all-to-all(f32[32,32,128]{2,1,0:T(8,128)S(1)} %broadcast_in_dim.2), channel_id=1, replica_groups=mesh['prow'=32,'pcol'=8] {'prow'}, dimensions={0} | all-to-all | bytes 1048576 | tf_op jit(solution)/shard_map/all_to_all | solution.py:23
  315.4 0.3 copy.7
  315.8 0.1 reshape.21
  315.9 0.0 copy-done
  315.9 0.4 fusion.7
  316.3 0.3 convolution_subtract_fusion.1
  316.6 0.4 fusion.6
  317.0 12.8 %convolution_subtract_fusion = f32[128,7168]{1,0:T(8,128)} fusion(f32[128,7168]{1,0:T(8,128)} %all_to_all.23, f32[7168,512]{0,1:T(8,128)} %all-gather.2.cloned.1.call-done, f32[128,256]{1,0:T(8,128)S(1)} %fusion.7, f32[128,256]{1,0:T(8,128)S(1)} %fusion.6), kind=kOutput, calls=%fused_computation | convolution fusion | flops 2819555328 | bytes 22282240 | tf_op jit(solution)/shard_map/dot_general | solution.py:15
  (5 shorter events, 0.2 us)
Async XLA Ops:
  6.5 231.8 %all-gather.2.cloned.1.call-start = ((), (), s32[]{:S(2)}) async-start(), calls=%async_computation.3 | async-start | bytes 16515072 | tf_op jit(solution)/shard_map/all_gather | solution.py:29
  261.9 54.0 %copy-start = (f32[2,256,256]{2,1,0:T(8,128)S(1)}, f32[2,256,256]{2,1,0:T(8,128)}, u32[]{:S(2)}) copy-start(f32[2,256,256]{2,1,0:T(8,128)} %param.5) | copy-start | bytes 1572868
Sparse Core Ops, SparseCore 0:
  9.1 229.0 all-gather.1
where the time goes:
time: 337 us
  blocking collectives  193 us (57%)
  waiting for transfers between devices  86.7 us (26%)
  matrix products  37.4 us (11%)
  between operations  13.5 us (4%)
  local copies, waits for them, and re-layouts  5.81 us (2%)
    all_to_all x1, blocking collectives, body(): lax.all_to_all(eigen_rows, 'prow', split_axis=1, concat_axis=0, tiled=True)  140 us
    all_gather x1, waiting for transfers between devices, body(): vectors = lax.all_gather(reflectors, 'pcol', axis=1, tiled=True)  86 us
    dot_general x6, matrix products, matmul(): jnp.dot(left, right, precision=precision, preferred_element_type=jnp.floa...  37.4 us
    all_to_all x1, blocking collectives, sum_over_prow(): lax.all_to_all(slices, 'prow', split_axis=0, concat_axis=0, tiled=True)  32.9 us
    all_to_all x1, blocking collectives, sum_over_prow(): lax.all_to_all(copies, 'prow', split_axis=0, concat_axis=0, tiled=True)  20.4 us
  transfers between devices with their start and end apart: 1, of which 1 were waited for; matrix products, arithmetic and copies ran while one was open for 0% of the time, Pallas kernels for 0%

commit v1 on v0

--- a/solution.py
+++ b/solution.py
@@ -26,7 +26,9 @@
 def body(eigen_rows, reflectors, tfactors):
     members = lax.axis_size("prow")
     width = tfactors.shape[1]
-    vectors = lax.all_gather(reflectors, "pcol", axis=1, tiled=True)
+    vectors = jnp.concatenate(
+        lax.all_to_all(jnp.stack([reflectors] * lax.axis_size("pcol")), "pcol", 0, 0), axis=1
+    )
     rows = lax.all_to_all(eigen_rows, "prow", split_axis=1, concat_axis=0, tiled=True)
     count = rows.shape[0]
     first_tri = upper_part(tfactors[0])

time: 337 us -> 512 us (1.52)
  waiting for transfers between devices: 86.7 us -> 310 us
  blocking collectives: 193 us -> 143 us
  between operations: 13.5 us -> 0.13 us
  local copies, waits for them, and re-layouts: 5.81 us -> 12.8 us
  starting transfers between devices: 0.01 us -> 5.49 us
    all_to_all x0 -> x1, waiting for transfers between devices: none -> 310 us  [body(): lax.all_to_all(jnp.stack([reflectors] * lax.axis_size('pcol')), 'pcol', 0...]
    all_gather x1 -> x0, waiting for transfers between devices: 86 us -> none  [body(): vectors = lax.all_gather(reflectors, 'pcol', axis=1, tiled=True)]
    all_to_all x1, blocking collectives: 140 us -> 101 us  [body(): lax.all_to_all(eigen_rows, 'prow', split_axis=1, concat_axis=0, tiled=True)]
    all_to_all x1, blocking collectives: 32.9 us -> 22.4 us  [sum_over_prow(): lax.all_to_all(slices, 'prow', split_axis=0, concat_axis=0, tiled=True)]
    another operation x0 -> x1, local copies, waits for them, and re-layouts: none -> 6.95 us  [body(): jnp.stack([reflectors] * lax.axis_size('pcol'))]
    all_to_all x0 -> x1, starting transfers between devices: none -> 5.49 us  [body(): lax.all_to_all(jnp.stack([reflectors] * lax.axis_size('pcol')), 'pcol', 0...]
where the time goes in v1:
time: 512 us; the launch traced here: 507 us
  waiting for transfers between devices  310 us (61%)
  blocking collectives  143 us (28%)
  matrix products  36.4 us (7%)
  local copies, waits for them, and re-layouts  12.8 us (2%)
  starting transfers between devices  5.49 us (1%)
    all_to_all x1, waiting for transfers between devices, body(): lax.all_to_all(jnp.stack([reflectors] * lax.axis_size('pcol')), 'pcol', 0...  310 us
    all_to_all x1, blocking collectives, body(): lax.all_to_all(eigen_rows, 'prow', split_axis=1, concat_axis=0, tiled=True)  101 us
    dot_general x6, matrix products, matmul(): jnp.dot(left, right, precision=precision, preferred_element_type=jnp.floa...  36.4 us
    all_to_all x1, blocking collectives, sum_over_prow(): lax.all_to_all(slices, 'prow', split_axis=0, concat_axis=0, tiled=True)  22.4 us
    all_to_all x1, blocking collectives, sum_over_prow(): lax.all_to_all(copies, 'prow', split_axis=0, concat_axis=0, tiled=True)  18.8 us
  transfers between devices with their start and end apart: 1, of which 1 were waited for; matrix products, arithmetic and copies ran while one was open for 0% of the time, Pallas kernels for 0%

profile of v1, /device:TPU:32, one launch (start us, length us, event | category | flops | bytes accessed | tf_op | source)
XLA Modules:
  0.0 507.3 jit_solution(14790434998226724096)
XLA Ops:
  0.0 0.0 copy-start.1
  0.0 101.5 %all_to_all.34 = f32[4,32,7168]{2,0,1:T(4,128)} all-to-all(f32[4,32,7168]{2,0,1:T(4,128)} %bitcast.22), channel_id=1, replica_groups=mesh['prow'=32,'pcol'=8] {'prow'}, dimensions={1} | all-to-all | bytes 7340032 | tf_op jit(solution)/shard_map/all_to_all | solution.py:32
  101.5 0.0 copy-done.1
  101.5 6.9 %stack.2 = f32[8,7168,64]{1,2,0:T(8,128)} broadcast(f32[7168,64]{0,1:T(8,128)S(1)} %copy-done.1), dimensions={1,2} | broadcast | bytes 16515072 | tf_op jit(solution)/shard_map/stack | solution.py:30
  108.5 5.5 %all-to-all-start.1 = ((f32[8,7168,64]{1,2,0:T(8,128)}), f32[8,7168,64]{1,2,0:T(8,128)}, u32[]{:S(2)}, u32[]{:S(2)}) async-start(f32[8,7168,64]{1,2,0:T(8,128)} %stack.2), calls=%async_computation.1 | async-start | bytes 29360128 | tf_op jit(solution)/shard_map/all_to_all | solution.py:30
  113.9 5.2 %all_to_all.26 = f32[128,7168]{1,0:T(8,128)} reshape(f32[32,4,7168]{2,1,0:T(4,128)} %bitcast.21) | data formatting | bytes 7340032 | tf_op jit(solution)/shard_map/all_to_all | solution.py:32
  119.2 309.7 %all-to-all-done.1 = f32[8,7168,64]{1,2,0:T(8,128)} async-done(((f32[8,7168,64]{1,2,0:T(8,128)}), f32[8,7168,64]{1,2,0:T(8,128)}, u32[]{:S(2)}, u32[]{:S(2)}) %all-to-all-start.1) | async-done | bytes 14680096 | tf_op jit(solution)/shard_map/all_to_all | solution.py:30
  428.9 0.0 copy-start
  428.9 11.9 %fusion = f32[256,256]{1,0:T(8,128)S(1)} fusion(f32[7168,512]{0,1:T(8,128)} %bitcast.3), kind=kOutput, calls=%fused_computation.1 | convolution fusion | flops 2818572288 | bytes 14942208 | tf_op jit(solution)/shard_map/dot_general | solution.py:15
  440.7 0.0 copy-done
  440.8 10.7 %fusion.17 = f32[128,512]{1,0:T(8,128)S(1)} fusion(f32[128,7168]{1,0:T(8,128)S(1)} %copy-done, f32[7168,512]{0,1:T(8,128)} %bitcast.3), kind=kOutput, calls=%fused_computation.24 | convolution fusion | flops 2818572288 | bytes 18612224 | tf_op jit(solution)/shard_map/dot_general | solution.py:15
  451.5 0.0 copy-start.2
  451.6 0.1 pad_maximum_fusion
  451.6 22.4 %all_to_all.35 = f32[32,32,128]{2,1,0:T(8,128)S(1)} all-to-all(f32[32,32,128]{2,1,0:T(8,128)S(1)} %pad_maximum_fusion), channel_id=1, replica_groups=mesh['prow'=32,'pcol'=8] {'prow'}, dimensions={0} | all-to-all | bytes 1048576 | tf_op jit(solution)/shard_map/all_to_all | solution.py:20
  474.1 0.1 broadcast_in_dim.2
  474.1 18.8 %all_to_all.36 = f32[32,32,128]{2,1,0:T(8,128)S(1)} all-to-all(f32[32,32,128]{2,1,0:T(8,128)S(1)} %broadcast_in_dim.2), channel_id=1, replica_groups=mesh['prow'=32,'pcol'=8] {'prow'}, dimensions={0} | all-to-all | bytes 1048576 | tf_op jit(solution)/shard_map/all_to_all | solution.py:23
  492.9 0.3 copy.9
  493.3 0.1 reshape.31
  493.4 0.0 copy-done.2
  493.4 0.4 fusion.7
  493.8 0.3 convolution_subtract_fusion.1
  494.1 0.4 fusion.6
  494.5 12.8 %convolution_subtract_fusion = f32[128,7168]{1,0:T(8,128)} fusion(f32[128,7168]{1,0:T(8,128)} %all_to_all.26, f32[7168,512]{0,1:T(8,128)} %bitcast.3, f32[128,256]{1,0:T(8,128)S(1)} %fusion.7, f32[128,256]{1,0:T(8,128)S(1)} %fusion.6), kind=kOutput, calls=%fused_computation | convolution fusion | flops 2819555328 | bytes 22282240 | tf_op jit(solution)/shard_map/dot_general | solution.py:15
  (5 shorter events, 0.2 us)
Async XLA Ops:
  0.0 101.5 %copy-start.1 = (f32[7168,64]{0,1:T(8,128)S(1)}, f32[7168,64]{0,1:T(8,128)}, u32[]{:S(2)}) copy-start(f32[7168,64]{0,1:T(8,128)} %param.4) | copy-start | bytes 5505028
  108.5 320.4 %all-to-all-start.1 = ((f32[8,7168,64]{1,2,0:T(8,128)}), f32[8,7168,64]{1,2,0:T(8,128)}, u32[]{:S(2)}, u32[]{:S(2)}) async-start(f32[8,7168,64]{1,2,0:T(8,128)} %stack.2), calls=%async_computation.1 | async-start | bytes 29360128 | tf_op jit(solution)/shard_map/all_to_all | solution.py:30
  428.9 11.9 %copy-start = (f32[128,7168]{1,0:T(8,128)S(1)}, f32[128,7168]{1,0:T(8,128)}, u32[]{:S(2)}) copy-start(f32[128,7168]{1,0:T(8,128)} %all_to_all.26) | copy-start | bytes 11010052
  451.5 41.9 %copy-start.2 = (f32[2,256,256]{2,1,0:T(8,128)S(1)}, f32[2,256,256]{2,1,0:T(8,128)}, u32[]{:S(2)}) copy-start(f32[2,256,256]{2,1,0:T(8,128)} %param.5) | copy-start | bytes 1572868
